TPU v7x, 32 devices: a whole 2x2x4 slice. The times are simulated.
32 devices in a mesh: rows: 2 (over x), cols: 16 (over z, y, core).
Axes of the slice: x: 2, y: 2, z: 4, core: 2. Of those that a mesh axis runs over, the one named last changes fastest.
Arguments:
- queries: bfloat16 [8192, 1024], P(('rows', 'cols')), may hold values from -1 to 1
- attn_out: bfloat16 [8192, 1024], P(('rows', 'cols')), may hold values from -6 to 6
- out_grad: bfloat16 [8192, 1024], P(('rows', 'cols')), may hold values from -96 to 96
- log_norm: float32 [8192, 8], P(('rows', 'cols')), may hold values from 7.5 to 8.5
- leaf_kv: bfloat16 [8192, 256], P(('rows', 'cols')), may hold values from -1 to 1
- root_kv: bfloat16 [2048, 256], P('cols'), may hold values from -1 to 1
- branch_kv: bfloat16 [4, 1024, 256], P('rows', 'cols'), may hold values from -1 to 1
- branch_len: int32 [4], replicated, may hold values from 256 to 1024, as said below
- segment_ids: int32 [32, 256], P(('rows', 'cols')), may hold values from 0 to 7, never falling along the last dimension, each value on 1 to 128 neighbouring positions
- segment_branch: int32 [32, 8], P(('rows', 'cols')), may hold values from 0 to 1
Outputs:
- query_grad: bfloat16 [8192, 1024], P(('rows', 'cols'))
- leaf_kv_grad: float32 [8192, 256], P(('rows', 'cols'))
- root_kv_grad: float32 [2048, 256], P('cols')
- branch_kv_grad: float32 [4, 1024, 256], P('rows', 'cols')
Inputs may be any that keep to these rules, and one draw needn't show every extreme that they name: `branch_len`: every branch has between 256 and 1024 live slots; some branch has exactly 1024 and some exactly 256. `segment_ids`: never falling along a device's tokens; each segment has 1 to 128 tokens, one exactly 128. `segment_branch`: a segment on row r extends branch r * 2 + value.
All inputs are finite; a program needn't handle non-finite values.
Results may differ from a plain program's by a relative error of at most 0.0041.
Values may be sent and summed in bfloat16 or wider, within the bound.
A program may use at most 64 MiB of HBM per device.

v0:
```python
from functools import partial

import jax
import jax.numpy as jnp
from jax import lax
from jax.sharding import PartitionSpec as P

HEADS = 8
HD = 128
BR_DEV = 2
SEGS = 8


def block_grads(query_heads, grad_heads, log_norm, row_delta, key_rows, allowed):
    scale = HD ** (-0.5)
    keys_part = key_rows[:, :HD]
    values_part = key_rows[:, HD:]
    scores = (
        jnp.einsum("thd,kd->thk", query_heads, keys_part, preferred_element_type=jnp.float32)
        * scale
    )
    weights = jnp.where(allowed[:, None, :], jnp.exp(scores - log_norm[:, :, None]), 0.0)
    dweight = jnp.einsum("thd,kd->thk", grad_heads, values_part, preferred_element_type=jnp.float32)
    dscore = weights * (dweight - row_delta[:, :, None])
    weight_b = weights.astype(jnp.bfloat16)
    dscore_b = dscore.astype(jnp.bfloat16)
    query_part = (
        jnp.einsum("thk,kd->thd", dscore_b, keys_part, preferred_element_type=jnp.float32) * scale
    )
    key_grad = (
        jnp.einsum("thk,thd->kd", dscore_b, query_heads, preferred_element_type=jnp.float32) * scale
    )
    value_grad = jnp.einsum("thk,thd->kd", weight_b, grad_heads, preferred_element_type=jnp.float32)
    return (query_part, jnp.concatenate([key_grad, value_grad], axis=1))


def sweep_keys(query_heads, grad_heads, log_norm, row_delta, key_rows, allowed_of):
    count_rows = key_rows.shape[0]
    block_rows = 512 if count_rows % 512 == 0 else count_rows

    def visit_block(query_sum, block_index):
        offset = block_index * block_rows
        key_block = lax.dynamic_slice_in_dim(key_rows, offset, block_rows, 0)
        query_part, key_grads = block_grads(
            query_heads, grad_heads, log_norm, row_delta, key_block, allowed_of(offset, block_rows)
        )
        return (query_sum + query_part, key_grads)

    start_sum = jnp.zeros(query_heads.shape, jnp.float32)
    query_sum, key_grads = lax.scan(
        visit_block, start_sum, jnp.arange(count_rows // block_rows, dtype=jnp.int32)
    )
    return (query_sum, key_grads.reshape(count_rows, key_rows.shape[1]))


def shards(
    queries,
    attn_out,
    out_grad,
    log_norm,
    leaf_kv,
    root_kv,
    branch_kv,
    branch_len,
    segment_ids,
    segment_branch,
):
    tokens = queries.shape[0]
    query_heads = queries.reshape(tokens, HEADS, HD)
    grad_heads = out_grad.reshape(tokens, HEADS, HD)
    out_heads = attn_out.reshape(tokens, HEADS, HD)
    row_delta = jnp.sum(grad_heads.astype(jnp.float32) * out_heads.astype(jnp.float32), axis=2)
    segment = segment_ids[0]
    seg_branch = segment_branch[0]
    token_branch = jnp.sum(
        jnp.where(
            segment[:, None] == jnp.arange(SEGS, dtype=jnp.int32)[None, :], seg_branch[None, :], 0
        ),
        axis=1,
    )
    row_index = lax.axis_index("rows")
    lengths = lax.dynamic_slice_in_dim(branch_len, row_index * BR_DEV, BR_DEV, 0)
    run_keys = partial(sweep_keys, query_heads, grad_heads, log_norm, row_delta)

    def every_key(offset, count_rows):
        return jnp.ones((tokens, count_rows), dtype=bool)

    query_part, piece_grads = run_keys(
        lax.all_gather(root_kv, "cols", axis=0, tiled=True), every_key
    )
    root_grads = piece_grads
    query_grad = query_part
    piece = lax.all_gather(branch_kv, "cols", axis=1, tiled=True)
    branch_query_grad = query_grad
    updates = []
    for slot in range(BR_DEV):

        def slot_allowed(offset, count_rows, slot=slot):
            slot_pos = offset + jnp.arange(count_rows, dtype=jnp.int32)
            return (token_branch == slot)[:, None] & (slot_pos < lengths[slot])[None, :]

        query_part, piece_grads = run_keys(piece[slot], slot_allowed)
        branch_query_grad = branch_query_grad + query_part
        updates.append(piece_grads)
    branch_grads = jnp.stack(updates)
    query_grad = branch_query_grad
    positions = jnp.arange(tokens, dtype=jnp.int32)

    def leaf_allowed(offset, count_rows):
        key_pos = offset + jnp.arange(count_rows, dtype=jnp.int32)
        return (segment[:, None] == segment[None, :]) & (key_pos[None, :] <= positions[:, None])

    leaf_part, leaf_grads = run_keys(leaf_kv, leaf_allowed)
    query_grad = query_grad + leaf_part
    branch_grad = lax.psum_scatter(branch_grads, "cols", scatter_dimension=1, tiled=True)
    row_whole = lax.psum(root_grads, "rows")
    root_grad = lax.psum_scatter(row_whole, "cols", scatter_dimension=0, tiled=True)
    return (
        query_grad.reshape(tokens, HEADS * HD).astype(jnp.bfloat16),
        leaf_grads,
        root_grad,
        branch_grad,
    )


def solution(mesh):
    in_specs = (
        P(("rows", "cols"), None),
        P(("rows", "cols"), None),
        P(("rows", "cols"), None),
        P(("rows", "cols"), None),
        P(("rows", "cols"), None),
        P("cols", None),
        P("rows", "cols", None),
        P(),
        P(("rows", "cols"), None),
        P(("rows", "cols"), None),
    )
    out_specs = (
        P(("rows", "cols"), None),
        P(("rows", "cols"), None),
        P("cols", None),
        P("rows", "cols", None),
    )
    return jax.shard_map(shards, mesh=mesh, in_specs=in_specs, out_specs=out_specs, check_vma=False)
```

profile of v0, /device:TPU:0, one launch (start us, length us, event | category | flops | bytes accessed | tf_op | source)
XLA Modules:
  0.0 288.9 jit_solution(9851445871758798752)
XLA Ops:
  8.8 1.2 copy.59
  10.0 1.2 copy.58
  11.3 1.2 copy.60
  14.1 36.6 %all-gather.5.cloned.1.call-done = bf16[2,1024,256]{2,1,0:T(8,128)(2,1)} async-done(((bf16[2,64,256]{2,1,0:T(8,128)(2,1)}), bf16[2,1024,256]{2,1,0:T(8,128)(2,1)}) %all-gather.5.cloned.1.call-update) | async-done | bytes 1048592 | tf_op jit(solution)/shard_map/all_gather | solution.py:93
  50.8 2.2 slice_bitcast_fusion.1
  53.0 1.1 broadcast.152.clone2
  54.1 24.9 %while.46 = (s32[]{:T(128)}, f32[256,8,128]{2,0,1:T(8,128)}, f32[2,512,256]{2,1,0:T(8,128)}, s32[256]{0:T(256)S(1)}, s32[2]{0:T(128)S(1)}, /*index=5*/s32[2]{0:T...) while((s32[]{:T(128)}, f32[256,8,128]{2,0,1:T(8,128)}, ...), condition=%wide.region_7.8_spmd.clone, body=%wide.region_6.7_spmd.clone.sunk | while | flops 1353778432 | bytes 27552528 | solution.py:50
  56.8 1.6 fusion.157
  58.4 1.0 fusion.160
  59.4 2.3 fusion.158
  62.5 2.7 fusion.159
  65.4 0.8 constant_dynamic-update-slice_fusion.8
  69.0 1.6 fusion.157
  70.6 1.0 fusion.160
  71.6 2.3 fusion.158
  74.7 3.1 %fusion.159 = f32[256,8,128]{2,0,1:T(8,128)} fusion(bf16[256,8,512]{0,2,1:T(8,128)(2,1)S(1)} %fusion.158, f32[256,8,128]{2,0,1:T(8,128)} %get-tuple-element.584, pred[]{:T(512)S(6)} %compare.11, bf16[1024,256]{1,0:T(8,128)(2,1)} %get-tuple-element.605, s32[]{:T(128)S(6)} %select_n.70), kind=kOutput, calls=%fused_computation.54.clone.1 | convolution fusion | flops 269221888 | bytes 4325381 | tf_op jit(solution)/shard_map/while/body/eval_jaxpr/thk,kd->thd/dot_general | solution.py:28
  78.1 0.8 constant_dynamic-update-slice_fusion.8
  78.9 10.9 %all-gather.3.cloned.1.call-done = bf16[2048,256]{1,0:T(8,128)(2,1)} async-done(((bf16[128,256]{1,0:T(8,128)(2,1)}), bf16[2048,256]{1,0:T(8,128)(2,1)}) %all-gather.3.cloned.1.call-update) | async-done | bytes 1048592 | tf_op jit(solution)/shard_map/all_gather | solution.py:89
  89.9 42.4 %while.44 = (s32[]{:T(128)}, f32[256,8,128]{2,0,1:T(8,128)}, f32[4,512,256]{2,1,0:T(8,128)}, s32[4]{0:T(128)S(1)}, bf16[2048,256]{1,0:T(8,128)(2,1)}, /*index=5*...) while((s32[]{:T(128)}, f32[256,8,128]{2,0,1:T(8,128)}, ...), condition=%wide.region_2.3_spmd.clone, body=%wide.region_1.2_spmd.clone.sunk | while | flops 1351548928 | bytes 27156720 | solution.py:50
  91.1 1.6 fusion.134
  92.7 0.9 fusion.136
  93.6 2.0 multiply_convert_fusion.3
  96.4 2.6 fusion.135
  99.3 0.8 constant_dynamic-update-slice_fusion.6
  101.4 1.6 fusion.134
  103.0 0.9 fusion.136
  103.9 2.0 multiply_convert_fusion.3
  105.9 0.8 fusion.137
  106.7 3.0 %fusion.135 = f32[256,8,128]{2,0,1:T(8,128)} fusion(bf16[512,256,8]{1,0,2:T(8,128)(2,1)S(1)} %multiply_convert_fusion.3, f32[256,8,128]{2,0,1:T(8,128)} %get-tuple-element.630, pred[]{:T(512)S(6)} %compare.9, bf16[2048,256]{1,0:T(8,128)(2,1)} %get-tuple-element.647, s32[]{:T(128)S(6)} %select_n.64), kind=kOutput, calls=%fused_computation.12.clone.1 | convolution fusion | flops 269221888 | bytes 4325381 | tf_op jit(solution)/shard_map/while/body/eval_jaxpr/thk,kd->thd/dot_general | solution.py:28
  110.0 0.8 constant_dynamic-update-slice_fusion.6
  112.1 1.6 fusion.134
  113.7 0.9 fusion.136
  114.6 2.0 multiply_convert_fusion.3
  116.6 0.8 fusion.137
  117.4 3.0 %fusion.135 = f32[256,8,128]{2,0,1:T(8,128)} fusion(bf16[512,256,8]{1,0,2:T(8,128)(2,1)S(1)} %multiply_convert_fusion.3, f32[256,8,128]{2,0,1:T(8,128)} %get-tuple-element.630, pred[]{:T(512)S(6)} %compare.9, bf16[2048,256]{1,0:T(8,128)(2,1)} %get-tuple-element.647, s32[]{:T(128)S(6)} %select_n.64), kind=kOutput, calls=%fused_computation.12.clone.1 | convolution fusion | flops 269221888 | bytes 4325381 | tf_op jit(solution)/shard_map/while/body/eval_jaxpr/thk,kd->thd/dot_general | solution.py:28
  120.7 0.8 constant_dynamic-update-slice_fusion.6
  122.8 1.6 fusion.134
  124.4 0.9 fusion.136
  125.3 2.0 multiply_convert_fusion.3
  128.1 3.0 %fusion.135 = f32[256,8,128]{2,0,1:T(8,128)} fusion(bf16[512,256,8]{1,0,2:T(8,128)(2,1)S(1)} %multiply_convert_fusion.3, f32[256,8,128]{2,0,1:T(8,128)} %get-tuple-element.630, pred[]{:T(512)S(6)} %compare.9, bf16[2048,256]{1,0:T(8,128)(2,1)} %get-tuple-element.647, s32[]{:T(128)S(6)} %select_n.64), kind=kOutput, calls=%fused_computation.12.clone.1 | convolution fusion | flops 269221888 | bytes 4325381 | tf_op jit(solution)/shard_map/while/body/eval_jaxpr/thk,kd->thd/dot_general | solution.py:28
  131.4 0.8 constant_dynamic-update-slice_fusion.6
  132.5 1.1 broadcast.152.clone2.1
  133.6 17.1 %while.45 = (s32[]{:T(128)}, f32[256,8,128]{2,0,1:T(8,128)S(1)}, f32[2,512,256]{2,1,0:T(8,128)}, s32[256]{0:T(256)S(1)}, s32[2]{0:T(128)S(1)}, /*index=5*/s32[2]...) while((s32[]{:T(128)}, f32[256,8,128]{2,0,1:T(8,128)S(1)}, ...), condition=%wide.region_5.6_spmd.clone, body=%wide.region_4.5_spmd.clone.sunk | while | flops 1353778432 | bytes 29649700 | solution.py:50
  135.0 1.6 fusion.145
  136.6 1.0 fusion.148
  137.7 1.4 fusion.146
  139.9 1.1 fusion.147
  141.3 0.8 constant_dynamic-update-slice_fusion.7
  143.5 1.6 fusion.145
  145.2 1.0 fusion.148
  146.2 1.4 fusion.146
  148.4 1.1 fusion.147
  149.8 0.9 constant_dynamic-update-slice_fusion.7
  150.7 3.0 %pad_maximum_fusion = f32[2,1024,256]{2,1,0:T(8,128)} fusion(f32[1,1024,256]{2,1,0:T(8,128)} %bitcast.248, f32[1,1024,256]{2,1,0:T(8,128)} %bitcast.247), kind=kLoop, calls=%fused_computation.70 | loop fusion | flops 524288 | bytes 4194304 | tf_op jit(solution)/shard_map/stack | solution.py:105
  155.9 0.8 copy.71
  156.7 1.6 copy.63
  158.3 1.3 copy.62
  159.6 1.6 copy.61
  161.2 32.0 %reduce-scatter.5.cloned.1.call-done = f32[128,256]{1,0:T(8,128)} async-done(((f32[2048,256]{1,0:T(8,128)}), f32[128,256]{1,0:T(8,128)}) %reduce-scatter.5.cloned.1.call-update) | async-done | bytes 131088 | tf_op jit(solution)/shard_map/reduce_scatter | solution.py:117
  193.2 2.5 fusion.60
  195.8 2.0 copy.70
  197.8 60.3 %reduce-scatter.3.cloned.1.call-done = f32[2,64,256]{2,1,0:T(8,128)} async-done(((f32[2,1024,256]{2,1,0:T(8,128)}), f32[2,64,256]{2,1,0:T(8,128)}) %reduce-scatter.3.cloned.1.call-update) | async-done | bytes 131088 | tf_op jit(solution)/shard_map/reduce_scatter | solution.py:115
  258.1 22.6 %all-reduce.2.cloned.1.call-done = f32[128,256]{1,0:T(8,128)} async-done(((f32[128,256]{1,0:T(8,128)}), f32[128,256]{1,0:T(8,128)}) %all-reduce.2.cloned.1.call-update) | async-done | bytes 131088 | tf_op jit(solution)/shard_map/psum | solution.py:116
  280.8 1.6 copy.135
  (80 shorter events, 20.1 us)
Async XLA Ops:
  7.2 43.6 %all-gather.5.cloned.1.call-start = ((), (), s32[]{:S(2)}) async-start(), calls=%async_computation.3 | async-start | bytes 1114112 | tf_op jit(solution)/shard_map/all_gather | solution.py:93
  7.9 82.0 %all-gather.3.cloned.1.call-start = ((), (), s32[]{:S(2)}) async-start(), calls=%async_computation.2 | async-start | bytes 1114112 | tf_op jit(solution)/shard_map/all_gather | solution.py:89
  8.6 184.6 %reduce-scatter.5.cloned.1.call-start = ((), (), s32[]{:S(2)}) async-start(), calls=%async_computation.5 | async-start | bytes 2228224 | tf_op jit(solution)/shard_map/reduce_scatter | solution.py:117
  8.7 45.3 %copy-start.1 = (f32[256,8]{0,1:T(8,128)S(1)}, f32[256,8]{0,1:T(8,128)}, u32[]{:S(2)}) copy-start(f32[256,8]{0,1:T(8,128)} %param.19) | copy-start | bytes 24580
  132.3 125.9 %reduce-scatter.3.cloned.1.call-start = ((), (), s32[]{:S(2)}) async-start(), calls=%async_computation.4 | async-start | bytes 2228224 | tf_op jit(solution)/shard_map/reduce_scatter | solution.py:115
  136.6 1.1 copy-start
  145.1 1.1 copy-start
  150.7 3.1 %copy-start.3 = (s32[1,256]{1,0:T(1,128)S(1)}, s32[1,256]{1,0:T(1,128)}, u32[]{:S(2)}) copy-start(s32[1,256]{1,0:T(1,128)} %param.24) | copy-start | bytes 3076
  150.7 3.2 %copy-start.2 = (bf16[256,256]{1,0:T(8,128)(2,1)S(1)}, bf16[256,256]{1,0:T(8,128)(2,1)}, u32[]{:S(2)}) copy-start(bf16[256,256]{1,0:T(8,128)(2,1)} %param.20) | copy-start | bytes 393220
  153.7 127.0 %all-reduce.2.cloned.1.call-start = ((), (), s32[]{:S(2)}) async-start(), calls=%async_computation.6 | async-start | bytes 262144 | tf_op jit(solution)/shard_map/psum | solution.py:116
Sparse Core Ops, SparseCore 0:
  10.2 40.5 all-gather.4
  52.9 36.8 all-gather.2
  132.4 60.7 reduce-scatter.4
  197.4 60.7 reduce-scatter.2
  260.3 20.4 all-reduce.1
where the time goes:
time: 290 us; the launch traced here: 289 us
  waiting for transfers between devices  164 us (57%)
  matrix products  66.6 us (23%)
  local copies, waits for them, and re-layouts  32.1 us (11%)
  between operations  13.9 us (5%)
  other arithmetic  6.25 us (2%)
  loops' own time  5.64 us (2%)
    reduce_scatter x1, waiting for transfers between devices, shards(): lax.psum_scatter(branch_grads, 'cols', scatter_dimension=1, tiled=True)  60.3 us
    all_gather x1, waiting for transfers between devices, shards(): piece = lax.all_gather(branch_kv, 'cols', axis=1, tiled=True)  36.6 us
    reduce_scatter x1, waiting for transfers between devices, shards(): lax.psum_scatter(row_whole, 'cols', scatter_dimension=0, tiled=True)  32 us
    psum x1, waiting for transfers between devices, shards(): row_whole = lax.psum(root_grads, 'rows')  22.6 us
    dot_general x9, matrix products, block_grads(): jnp.einsum('thk,kd->thd', dscore_b, keys_part, preferred_element_type=jnp...  22.4 us
    dot_general x9, matrix products, block_grads(): jnp.einsum('thd,kd->thk', grad_heads, values_part, preferred_element_type...  15.8 us
    dot_general x9, matrix products, block_grads(): jnp.einsum('thd,kd->thk', query_heads, keys_part, preferred_element_type=...  13.5 us
    all_gather x1, waiting for transfers between devices, shards(): lax.all_gather(root_kv, 'cols', axis=0, tiled=True)  10.9 us
  transfers between devices with their start and end apart: 5, of which 5 were waited for; matrix products, arithmetic and copies ran while one was open for 22% of the time, Pallas kernels for 0%

commit v1 on v0

v1 whole, which is shorter than its diff:
```python
import functools

import jax
import jax.numpy as jnp
from jax import lax
from jax.experimental import pallas as pl
from jax.experimental.pallas import tpu as pltpu
from jax.sharding import PartitionSpec as P

HEADS = 8
HD = 128
KB = 256
MESH = pl.DeviceIdType.MESH
F32 = jnp.float32
BF16 = jnp.bfloat16
LOG2E = 1.4426950408889634
VMEM = pl.BlockSpec(memory_space=pltpu.VMEM)
SMEM = pl.BlockSpec(memory_space=pltpu.SMEM)


def split_cols(cols):
    core = 2 if cols % 2 == 0 else 1
    chips = cols // core
    outer = 4 if chips % 4 == 0 else chips
    return outer, chips // outer, core


class Place:
    def __init__(self, cols):
        self.O, self.I, self.C = split_cols(cols)
        self.row = lax.axis_index("rows")
        me = lax.axis_index("cols")
        self.c = lax.rem(me, self.C)
        chip = me // self.C
        self.y = lax.rem(chip, self.I)
        self.z = chip // self.I

    def index(self, dz, dy, dc):
        z = lax.rem(self.z + dz + self.O, self.O)
        y = lax.rem(self.y + dy + self.I, self.I)
        c = lax.rem(self.c + dc + self.C, self.C)
        return (z * self.I + y) * self.C + c

    def dev(self, dz, dy, dc):
        return (self.row, self.index(dz, dy, dc))

    def greet(self, rows=1):
        sem = pltpu.get_barrier_semaphore()
        peers = [self.dev(d, 0, 0) for d in range(1, self.O)]
        peers += [self.dev(0, d, 0) for d in range(1, self.I)]
        peers += [self.dev(0, 0, d) for d in range(1, self.C)]
        for d in range(1, rows):
            peers.append((lax.rem(self.row + d, rows), lax.axis_index("cols")))
        for peer in peers:
            pl.semaphore_signal(sem, inc=1, device_id=peer, device_id_type=MESH)
        pl.semaphore_wait(sem, len(peers))


def gather_kernel(cols, root, branch, root_all, branch_all, zs, zr, ys, yr, cs, cr):
    at = Place(cols)
    O, I, C = at.O, at.I, at.C
    rb = root.shape[0]
    bb = branch.shape[1]

    def parts(i):
        return (
            root_all.at[pl.ds(pl.multiple_of(i * rb, rb), rb)],
            branch_all.at[:, pl.ds(pl.multiple_of(i * bb, bb), bb)],
        )

    sent = []

    def send(src, i, dev, ss, rs, slot):
        dst = parts(i)
        for k in range(2):
            cp = pltpu.make_async_remote_copy(
                src_ref=src[k], dst_ref=dst[k], send_sem=ss.at[slot, k], recv_sem=rs.at[slot, k],
                device_id=dev, device_id_type=MESH,
            )
            cp.start()
            sent.append(cp)

    def arrived(i, dev, ss, rs, slot):
        dst = parts(i)
        for k in range(2):
            pltpu.make_async_remote_copy(
                src_ref=dst[k], dst_ref=dst[k], send_sem=ss.at[slot, k], recv_sem=rs.at[slot, k],
                device_id=dev, device_id_type=MESH,
            ).wait_recv()

    at.greet()
    own = (root, branch)
    me = at.index(0, 0, 0)
    for dz in range(1, O):
        send(own, me, at.dev(dz, 0, 0), zs, zr, dz)
    for dy in range(1, I):
        send(own, me, at.dev(0, dy, 0), ys, yr, dy * O)
    for dc in range(1, C):
        send(own, me, at.dev(0, 0, dc), cs, cr, 0)
    mine = parts(me)
    mine[0][...] = root[...]
    mine[1][...] = branch[...]
    order = sorted(range(1, O), key=lambda d: min(d, O - d))
    for dz in order:
        i = at.index(-dz, 0, 0)
        arrived(i, at.dev(dz, 0, 0), zs, zr, dz)
        for dy in range(1, I):
            send(parts(i), i, at.dev(0, dy, 0), ys, yr, dy * O + dz)
        for dc in range(1, C):
            send(parts(i), i, at.dev(0, 0, dc), cs, cr, dz)
    for dz in [0] + order:
        for dy in range(1, I):
            i = at.index(-dz, -dy, 0)
            arrived(i, at.dev(0, dy, 0), ys, yr, dy * O + dz)
            for dc in range(1, C):
                send(parts(i), i, at.dev(0, 0, dc), cs, cr, dy * O + dz)
    for dc in range(1, C):
        for dy in range(I):
            for dz in [0] + order:
                arrived(at.index(-dz, -dy, -dc), at.dev(0, 0, dc), cs, cr, dy * O + dz)
    for cp in sent:
        cp.wait_send()


def gather(cols, root, branch):
    O, I, C = split_cols(cols)
    slots = O * I
    return pl.pallas_call(
        functools.partial(gather_kernel, cols),
        out_shape=(
            jax.ShapeDtypeStruct((root.shape[0] * cols, root.shape[1]), root.dtype),
            jax.ShapeDtypeStruct((branch.shape[0], branch.shape[1] * cols, branch.shape[2]), branch.dtype),
        ),
        in_specs=[VMEM] * 2,
        out_specs=(VMEM, VMEM),
        scratch_shapes=[pltpu.SemaphoreType.DMA((O, 2))] * 2 + [pltpu.SemaphoreType.DMA((slots, 2))] * 4,
        compiler_params=pltpu.CompilerParams(
            collective_id=0, has_side_effects=True, vmem_limit_bytes=16 << 20
        ),
        name="gather_kv",
    )(root, branch)


def reduce_kernel(
    rows, cols, root, branch, root_out, branch_out,
    rx1r, rx1b, s1, tx2, rx2, s2, tx3, rx3, rx4,
    a_s, a_r, b_s, b_r, c_s, c_r, d_s, d_r,
):
    at = Place(cols)
    O, I, C = at.O, at.I, at.C
    rb = root_out.shape[0]
    nb, bb, kw = branch_out.shape
    bf = nb * bb

    def parts(i):
        return (
            root.at[pl.ds(pl.multiple_of(i * rb, rb), rb)],
            branch.at[:, pl.ds(pl.multiple_of(i * bb, bb), bb)],
        )

    def copy(src, dst, ss, rs, dev):
        return pltpu.make_async_remote_copy(
            src_ref=src, dst_ref=dst, send_sem=ss, recv_sem=rs, device_id=dev, device_id_type=MESH
        )

    at.greet(rows)
    order = sorted(range(1, O), key=lambda d: -min(d, O - d)) + [0]
    pairs = [(dy, dz) for dy in list(range(1, I)) + [0] for dz in order]
    first = {}
    for dy, dz in pairs:
        slot = dy * O + dz
        for dc in range(1, C):
            src = parts(at.index(dz, dy, dc))
            dev = at.dev(0, 0, dc)
            first[dy, dz] = (
                copy(src[0], rx1r.at[slot], a_s.at[slot, 0], a_r.at[slot, 0], dev),
                copy(src[1], rx1b.at[slot], a_s.at[slot, 1], a_r.at[slot, 1], dev),
            )
            for cp in first[dy, dz]:
                cp.start()
    second = {}
    for dy, dz in pairs:
        slot = dy * O + dz
        own = parts(at.index(dz, dy, 0))
        r = own[0][...]
        b = own[1][...].reshape(bf, kw)
        if C > 1:
            for cp in first[dy, dz]:
                cp.wait_recv()
            r = r + rx1r[slot]
            b = b + rx1b[slot].reshape(bf, kw)
        if dy == 0:
            s1[dz, 0:rb] = r
            s1[dz, rb : rb + bf] = b
        else:
            tx2[slot - O, 0:rb] = r.astype(BF16)
            tx2[slot - O, rb : rb + bf] = b.astype(BF16)
            second[dy, dz] = copy(
                tx2.at[slot - O], rx2.at[slot - O], b_s.at[slot], b_r.at[slot], at.dev(0, dy, 0)
            )
            second[dy, dz].start()
    third = {}
    for dz in order:
        total = s1[dz]
        for dy in range(1, I):
            second[dy, dz].wait_recv()
            total = total + rx2[dy * O + dz - O].astype(F32)
        if dz == 0:
            s2[...] = total
        else:
            tx3[dz - 1] = total.astype(BF16)
            third[dz] = copy(
                tx3.at[dz - 1], rx3.at[dz - 1], c_s.at[dz], c_r.at[dz], at.dev(dz, 0, 0)
            )
            third[dz].start()
    total = s2[...]
    for dz in order[::-1][1:]:
        third[dz].wait_recv()
        total = total + rx3[dz - 1].astype(F32)
    branch_out[...] = total[rb : rb + bf].reshape(nb, bb, kw)
    rx4[at.row] = total[0:rb]
    fourth = []
    for dr in range(1, rows):
        dev = (lax.rem(at.row + dr, rows), lax.axis_index("cols"))
        cp = copy(rx4.at[at.row], rx4.at[at.row], d_s.at[dr], d_r.at[dr], dev)
        cp.start()
        fourth.append(cp)
    for dr in range(1, rows):
        row = lax.rem(at.row + rows - dr, rows)
        copy(rx4.at[row], rx4.at[row], d_s.at[dr], d_r.at[dr], (row, lax.axis_index("cols"))).wait_recv()
    out = rx4[0]
    for k in range(1, rows):
        out = out + rx4[k]
    root_out[...] = out
    for cps in first.values():
        for cp in cps:
            cp.wait_send()
    for cp in list(second.values()) + list(third.values()) + fourth:
        cp.wait_send()


def reduce(rows, cols, root, branch):
    O, I, C = split_cols(cols)
    slots = O * I
    rb = root.shape[0] // cols
    nb, blen, kw = branch.shape
    bb = blen // cols
    full = rb + nb * bb
    rest = max(slots - O, 1)
    dma = pltpu.SemaphoreType.DMA
    return pl.pallas_call(
        functools.partial(reduce_kernel, rows, cols),
        out_shape=(
            jax.ShapeDtypeStruct((rb, kw), F32),
            jax.ShapeDtypeStruct((nb, bb, kw), F32),
        ),
        in_specs=[VMEM] * 2,
        out_specs=(VMEM, VMEM),
        scratch_shapes=[
            pltpu.VMEM((slots, rb, kw), F32),
            pltpu.VMEM((slots, nb, bb, kw), F32),
            pltpu.VMEM((O, full, kw), F32),
            pltpu.VMEM((rest, full, kw), BF16),
            pltpu.VMEM((rest, full, kw), BF16),
            pltpu.VMEM((full, kw), F32),
            pltpu.VMEM((max(O - 1, 1), full, kw), BF16),
            pltpu.VMEM((max(O - 1, 1), full, kw), BF16),
            pltpu.VMEM((rows, rb, kw), F32),
            dma((slots, 2)), dma((slots, 2)), dma((slots,)), dma((slots,)),
            dma((O,)), dma((O,)), dma((rows,)), dma((rows,)),
        ],
        compiler_params=pltpu.CompilerParams(
            collective_id=1, has_side_effects=True, vmem_limit_bytes=32 << 20
        ),
        name="reduce_grads",
    )(root, branch)


def dot(a, b):
    return jnp.dot(a, b, preferred_element_type=F32)


def attend_kernel(
    lens_ref, segb_ref, q, o, g, ln_t, leaf, root, branch, seg,
    dq, leaf_g, root_g, branch_g,
    qt, gt, qs, gs, qt2, gt2, qs2, gs2, dqt, dst, pt, l2, delta,
):
    tok = q.shape[0]
    scale = HD ** (-0.5)
    nb = branch.shape[0]
    blen = branch.shape[1]
    row = lax.axis_index("rows")
    seg_row = seg[...]
    tb = jnp.zeros(seg_row.shape, jnp.int32)
    for s in range(segb_ref.shape[1]):
        tb = jnp.where(seg_row == s, segb_ref[0, s], tb)
    lens = [lens_ref[row * nb + b] for b in range(nb)]
    length = jnp.zeros(seg_row.shape, jnp.int32)
    for b in range(nb):
        length = jnp.where(tb == b, lens[b], length)
    tb_f = jnp.broadcast_to(tb.astype(F32), (HD, tok))
    tb_c = tb_f.T
    l2[...] = ln_t[...] * LOG2E
    for h in range(HEADS):
        hd = slice(h * HD, (h + 1) * HD)
        ht = slice(h * tok, (h + 1) * tok)
        qh = q[:, hd]
        gh = g[:, hd]
        qht = qh.T
        ght = gh.T
        delta[h : h + 1, :] = jnp.sum((gh.astype(F32) * o[:, hd].astype(F32)).T, axis=0, keepdims=True)
        qs[ht, :] = qh
        gs[ht, :] = gh
        qt[:, ht] = qht
        gt[:, ht] = ght
        for b in range(nb):
            bd = slice(b * HD, (b + 1) * HD)
            qs2[ht, bd] = jnp.where(tb_c == b, qh.astype(F32), 0.0).astype(BF16)
            gs2[ht, bd] = jnp.where(tb_c == b, gh.astype(F32), 0.0).astype(BF16)
            qt2[bd, ht] = jnp.where(tb_f == b, qht.astype(F32), 0.0).astype(BF16)
            gt2[bd, ht] = jnp.where(tb_f == b, ght.astype(F32), 0.0).astype(BF16)

    def block(k, v, qtr, gtr, qsr, gsr, allowed):
        for h in range(HEADS):
            ht = slice(h * tok, (h + 1) * tok)
            w = jnp.exp2(dot(k, qtr[:, ht]) * (scale * LOG2E) - l2[h : h + 1, :])
            if allowed is not None:
                w = jnp.where(allowed, w, 0.0)
            d = w * (dot(v, gtr[:, ht]) - delta[h : h + 1, :])
            pt[:, ht] = w.astype(BF16)
            dst[:, ht] = d.astype(BF16)
        ds = dst[...]
        return dot(ds, qsr[...]) * scale, dot(pt[...], gsr[...]), dot(k.T, ds)

    iota_k = lax.broadcasted_iota(jnp.int32, (tok, tok), 0)
    iota_t = lax.broadcasted_iota(jnp.int32, (tok, tok), 1)
    seg_b = jnp.broadcast_to(seg_row.astype(F32), (tok, tok))
    dk, dv, dqp = block(
        leaf[:, :HD], leaf[:, HD:], qt, gt, qs, gs, (seg_b == seg_b.T) & (iota_k <= iota_t)
    )
    leaf_g[:, :HD] = dk
    leaf_g[:, HD:] = dv
    dqt[...] = dqp

    longest = functools.reduce(jnp.maximum, lens)

    @pl.loop(0, blen // KB)
    def _(i):
        at = pl.ds(pl.multiple_of(i * KB, KB), KB)

        @pl.when(i * KB < longest)
        def _():
            pos = i * KB + lax.broadcasted_iota(jnp.int32, (KB, tok), 0)
            k = jnp.concatenate([branch[b, at, :HD] for b in range(nb)], axis=1)
            v = jnp.concatenate([branch[b, at, HD:] for b in range(nb)], axis=1)
            dk, dv, dqp = block(k, v, qt2, gt2, qs2, gs2, pos < length)
            for b in range(nb):
                bd = slice(b * HD, (b + 1) * HD)
                branch_g[b, at, :HD] = dk[:, bd]
                branch_g[b, at, HD:] = dv[:, bd]
            for h in range(HEADS):
                ht = slice(h * tok, (h + 1) * tok)
                part = dqp[:HD, ht]
                for b in range(1, nb):
                    part = jnp.where(tb_f == b, dqp[b * HD : (b + 1) * HD, ht], part)
                dqt[:, ht] += part

        @pl.when(i * KB >= longest)
        def _():
            for b in range(nb):
                branch_g[b, at, :] = jnp.zeros((KB, 2 * HD), F32)

    @pl.loop(0, root.shape[0] // KB)
    def _(i):
        at = pl.ds(pl.multiple_of(i * KB, KB), KB)
        dk, dv, dqp = block(root[at, :HD], root[at, HD:], qt, gt, qs, gs, None)
        root_g[at, :HD] = dk
        root_g[at, HD:] = dv
        dqt[...] += dqp

    for h in range(HEADS):
        dq[:, h * HD : (h + 1) * HD] = (dqt[:, h * tok : (h + 1) * tok].T * scale).astype(BF16)


def attend(lens, segb, q, o, g, ln_t, leaf, root, branch, seg):
    tok = q.shape[0]
    n = tok * HEADS
    nb = branch.shape[0]
    return pl.pallas_call(
        attend_kernel,
        out_shape=(
            jax.ShapeDtypeStruct(q.shape, BF16),
            jax.ShapeDtypeStruct(leaf.shape, F32),
            jax.ShapeDtypeStruct(root.shape, F32),
            jax.ShapeDtypeStruct(branch.shape, F32),
        ),
        in_specs=[SMEM] * 2 + [VMEM] * 8,
        out_specs=(VMEM,) * 4,
        scratch_shapes=[
            pltpu.VMEM((HD, n), BF16), pltpu.VMEM((HD, n), BF16),
            pltpu.VMEM((n, HD), BF16), pltpu.VMEM((n, HD), BF16),
            pltpu.VMEM((nb * HD, n), BF16), pltpu.VMEM((nb * HD, n), BF16),
            pltpu.VMEM((n, nb * HD), BF16), pltpu.VMEM((n, nb * HD), BF16),
            pltpu.VMEM((HD, n), F32),
            pltpu.VMEM((KB, n), BF16), pltpu.VMEM((KB, n), BF16),
            pltpu.VMEM((HEADS, tok), F32), pltpu.VMEM((HEADS, tok), F32),
        ],
        compiler_params=pltpu.CompilerParams(vmem_limit_bytes=48 << 20),
        name="attend_grads",
    )(lens, segb, q, o, g, ln_t, leaf, root, branch, seg)


def shards(rows, cols, q, o, g, log_norm, leaf, root, branch, lens, seg, segb):
    root_all, branch_all = gather(cols, root, branch)
    dq, leaf_g, root_g, branch_g = attend(
        lens, segb, q, o, g, log_norm.T, leaf, root_all, branch_all, seg
    )
    root_grad, branch_grad = reduce(rows, cols, root_g, branch_g)
    return dq, leaf_g, root_grad, branch_grad


def solution(mesh):
    both = P(("rows", "cols"), None)
    in_specs = (
        both, both, both, both, both, P("cols", None), P("rows", "cols", None), P(), both, both,
    )
    out_specs = (both, both, P("cols", None), P("rows", "cols", None))
    body = functools.partial(shards, mesh.shape["rows"], mesh.shape["cols"])
    return jax.shard_map(body, mesh=mesh, in_specs=in_specs, out_specs=out_specs, check_vma=False)
```

time: 290 us -> 85.8 us (0.30)
  waiting for transfers between devices: 164 us -> 0 us
  Pallas kernels: 0 us -> 73.4 us
  matrix products: 66.6 us -> 0 us
  local copies, waits for them, and re-layouts: 32.1 us -> 11.3 us
  between operations: 13.9 us -> 0.67 us
  other arithmetic: 6.25 us -> 0 us
  loops' own time: 5.64 us -> 0 us
    reduce_scatter x2 -> x0, waiting for transfers between devices: 92.4 us -> none  [the longest x1 60.3 us: shards(): lax.psum_scatter(branch_grads, 'cols', scatter_dimension=1, tiled=True)]
    pallas_call x0 -> x3, Pallas kernels: none -> 73.4 us  [the longest x1 30.8 us: reduce(): pl.pallas_call(functools.partial(reduce_kernel, rows, cols), out_shape=(j...]
    dot_general x45 -> x0, matrix products: 66.6 us -> none  [the longest x9 22.4 us: block_grads(): jnp.einsum('thk,kd->thd', dscore_b, keys_part, preferred_element_type=jnp...]
    all_gather x2 -> x0, waiting for transfers between devices: 47.5 us -> none  [the longest x1 36.6 us: shards(): piece = lax.all_gather(branch_kv, 'cols', axis=1, tiled=True)]
    psum x1 -> x0, waiting for transfers between devices: 22.6 us -> none  [shards(): row_whole = lax.psum(root_grads, 'rows')]
    dynamic_update_slice x16 -> x0, local copies, waits for them, and re-layouts: 8.34 us -> none  [sweep_keys(): lax.scan(visit_block, start_sum, jnp.arange(count_rows // block_rows, dty...]
    another operation x3 -> x0, loops' own time: 5.64 us -> none  [sweep_keys(): lax.scan(visit_block, start_sum, jnp.arange(count_rows // block_rows, dty...]
    dynamic_slice x9 -> x0, local copies, waits for them, and re-layouts: 5.5 us -> none  [the longest x8 4.77 us: sweep_keys(): lax.scan(visit_block, start_sum, jnp.arange(count_rows // block_rows, dty...]
  transfers between devices with their start and end apart: 5 -> 0, of which waited for: 5 -> 0; matrix products, arithmetic and copies ran while one was open for 22% -> 0% of each run, Pallas kernels for 0% -> 0%
where the time goes in v1:
time: 85.8 us; the launch traced here: 85.3 us
  Pallas kernels  73.4 us (86%)
  local copies, waits for them, and re-layouts  11.3 us (13%)
    pallas_call x1, Pallas kernels, reduce(): pl.pallas_call(functools.partial(reduce_kernel, rows, cols), out_shape=(j...  30.8 us
    pallas_call x1, Pallas kernels, gather(): pl.pallas_call(functools.partial(gather_kernel, cols), out_shape=(jax.Sha...  22.3 us
    pallas_call x1, Pallas kernels, attend(): pl.pallas_call(attend_kernel, out_shape=(jax.ShapeDtypeStruct(q.shape, BF...  20.2 us
    unnamed x24, local copies, waits for them, and re-layouts  11.3 us

profile of v1, /device:TPU:0, one launch (start us, length us, event | category | flops | bytes accessed | tf_op | source)
XLA Modules:
  0.0 85.3 jit_solution(9845989428754885246)
XLA Ops:
  0.6 0.0 copy-start.5
  0.6 0.8 copy-done.5
  1.5 0.0 copy-start.6
  1.5 0.8 copy-done.6
  2.3 22.3 %gather_kv.1 = (bf16[2048,256]{1,0:T(8,128)(2,1)S(1)}, bf16[2,1024,256]{2,1,0:T(8,128)(2,1)S(1)}) custom-call(bf16[128,256]{1,0:T(8,128)(2,1)S(1)} %copy-done.5, bf16[2,64,256]{2,1,0:T(8,128)(2,1)S(1)} %copy-done.6), custom_call_target="tpu_custom_call" | custom-call | tf_op jit(solution)/shard_map/gather_kv/pallas_call | solution.py:128
  24.7 0.0 copy-start.1
  24.7 1.0 %copy-done.1 = bf16[256,1024]{1,0:T(8,128)(2,1)S(1)} copy-done((bf16[256,1024]{1,0:T(8,128)(2,1)S(1)}, bf16[256,1024]{1,0:T(8,128)(2,1)}, u32[]{:S(2)}) %copy-start.1) | copy-done | bytes 524312
  25.7 0.0 copy-start.2
  25.7 1.0 %copy-done.2 = bf16[256,1024]{1,0:T(8,128)(2,1)S(1)} copy-done((bf16[256,1024]{1,0:T(8,128)(2,1)S(1)}, bf16[256,1024]{1,0:T(8,128)(2,1)}, u32[]{:S(2)}) %copy-start.2) | copy-done | bytes 524312
  26.8 0.0 copy-start.3
  26.8 1.0 %copy-done.3 = bf16[256,1024]{1,0:T(8,128)(2,1)S(1)} copy-done((bf16[256,1024]{1,0:T(8,128)(2,1)S(1)}, bf16[256,1024]{1,0:T(8,128)(2,1)}, u32[]{:S(2)}) %copy-start.3) | copy-done | bytes 524312
  27.8 0.0 copy-start.4
  27.8 0.9 %copy-done.4 = bf16[256,256]{1,0:T(8,128)(2,1)S(1)} copy-done((bf16[256,256]{1,0:T(8,128)(2,1)S(1)}, bf16[256,256]{1,0:T(8,128)(2,1)}, u32[]{:S(2)}) %copy-start.4) | copy-done | bytes 131096
  28.7 0.0 copy-start.7
  28.7 0.7 copy-done.7
  29.4 0.0 copy-start.8
  29.4 0.7 copy-done.8
  30.1 0.0 copy-start.9
  30.1 0.7 copy-done.9
  30.7 0.0 copy-start.10
  30.7 0.7 copy-done.10
  31.4 20.2 %attend_grads.1 = (bf16[256,1024]{1,0:T(8,128)(2,1)}, f32[256,256]{1,0:T(8,128)}, f32[2048,256]{1,0:T(8,128)S(1)}, f32[2,1024,256]{2,1,0:T(8,128)}) custom-call(s32[4]{0:T(128)S(1)} %copy-done.9, s32[1,8]{1,0:T(1,128)S(1)} %copy-done.10, bf16[256,1024]{1,0:T(8,128)(2,1)S(1)} %copy-done.1, bf16[256,1024]{1,0:T(8,128)(2,1)S(1)} %copy-done.2, ...), custom_call_target="tpu_custom_call" | custom-call | tf_op jit(solution)/shard_map/attend_grads/pallas_call | solution.py:389
  51.6 0.0 copy-start
  51.6 1.6 %copy-done = f32[2,1024,256]{2,1,0:T(8,128)S(1)} copy-done((f32[2,1024,256]{2,1,0:T(8,128)S(1)}, f32[2,1024,256]{2,1,0:T(8,128)}, u32[]{:S(2)}) %copy-start) | copy-done | bytes 2097176
  53.2 30.8 %reduce_grads.1 = (f32[128,256]{1,0:T(8,128)S(1)}, f32[2,64,256]{2,1,0:T(8,128)S(1)}) custom-call(f32[2048,256]{1,0:T(8,128)S(1)} %get-tuple-element.16.root, f32[2,1024,256]{2,1,0:T(8,128)S(1)} %copy-done), custom_call_target="tpu_custom_call" | custom-call | tf_op jit(solution)/shard_map/reduce_grads/pallas_call | solution.py:251
  84.0 0.7 copy.16
  84.7 0.7 copy.17
Async XLA Ops:
  0.6 0.8 copy-start.5
  1.5 0.8 copy-start.6
  24.7 1.0 %copy-start.1 = (bf16[256,1024]{1,0:T(8,128)(2,1)S(1)}, bf16[256,1024]{1,0:T(8,128)(2,1)}, u32[]{:S(2)}) copy-start(bf16[256,1024]{1,0:T(8,128)(2,1)} %q.1) | copy-start | bytes 1572868
  25.7 1.0 %copy-start.2 = (bf16[256,1024]{1,0:T(8,128)(2,1)S(1)}, bf16[256,1024]{1,0:T(8,128)(2,1)}, u32[]{:S(2)}) copy-start(bf16[256,1024]{1,0:T(8,128)(2,1)} %o.1) | copy-start | bytes 1572868
  26.8 1.0 %copy-start.3 = (bf16[256,1024]{1,0:T(8,128)(2,1)S(1)}, bf16[256,1024]{1,0:T(8,128)(2,1)}, u32[]{:S(2)}) copy-start(bf16[256,1024]{1,0:T(8,128)(2,1)} %g.1) | copy-start | bytes 1572868
  27.8 0.9 %copy-start.4 = (bf16[256,256]{1,0:T(8,128)(2,1)S(1)}, bf16[256,256]{1,0:T(8,128)(2,1)}, u32[]{:S(2)}) copy-start(bf16[256,256]{1,0:T(8,128)(2,1)} %leaf.1) | copy-start | bytes 393220
  28.7 0.7 copy-start.7
  29.4 0.7 copy-start.8
  30.1 0.7 copy-start.9
  30.7 0.7 copy-start.10
  51.6 1.6 %copy-start = (f32[2,1024,256]{2,1,0:T(8,128)S(1)}, f32[2,1024,256]{2,1,0:T(8,128)}, u32[]{:S(2)}) copy-start(f32[2,1024,256]{2,1,0:T(8,128)} %get-tuple-element.17.branch) | copy-start | bytes 6291460

commit v2 on v0

v2 whole, which is shorter than its diff:
```python
import functools

import jax
import jax.numpy as jnp
from jax import lax
from jax.experimental import pallas as pl
from jax.experimental.pallas import tpu as pltpu
from jax.sharding import PartitionSpec as P

HEADS = 8
HD = 128
KB = 256
MESH = pl.DeviceIdType.MESH
F32 = jnp.float32
BF16 = jnp.bfloat16
LOG2E = 1.4426950408889634
VMEM = pl.BlockSpec(memory_space=pltpu.VMEM)
SMEM = pl.BlockSpec(memory_space=pltpu.SMEM)


def split_cols(cols):
    core = 2 if cols % 2 == 0 else 1
    chips = cols // core
    outer = 4 if chips % 4 == 0 else chips
    return outer, chips // outer, core


class Place:
    def __init__(self, cols):
        self.O, self.I, self.C = split_cols(cols)
        self.row = lax.axis_index("rows")
        me = lax.axis_index("cols")
        self.c = lax.rem(me, self.C)
        chip = me // self.C
        self.y = lax.rem(chip, self.I)
        self.z = chip // self.I

    def index(self, dz, dy, dc):
        z = lax.rem(self.z + dz + self.O, self.O)
        y = lax.rem(self.y + dy + self.I, self.I)
        c = lax.rem(self.c + dc + self.C, self.C)
        return (z * self.I + y) * self.C + c

    def dev(self, dz, dy, dc):
        return (self.row, self.index(dz, dy, dc))

    def greet(self, rows=1):
        sem = pltpu.get_barrier_semaphore()
        peers = [self.dev(d, 0, 0) for d in range(1, self.O)]
        peers += [self.dev(0, d, 0) for d in range(1, self.I)]
        peers += [self.dev(0, 0, d) for d in range(1, self.C)]
        for d in range(1, rows):
            peers.append((lax.rem(self.row + d, rows), lax.axis_index("cols")))
        for peer in peers:
            pl.semaphore_signal(sem, inc=1, device_id=peer, device_id_type=MESH)
        pl.semaphore_wait(sem, len(peers))


def dot(a, b):
    return jnp.dot(a, b, preferred_element_type=F32)


def fused_kernel(
    rows, cols,
    lens_ref, segb_ref, q_in, o_in, g_in, ln_t, leaf_in, root, branch, seg,
    dq, leaf_g, root_out, branch_out,
    q, o, g, leaf, root_all, branch_all, root_g, branch_g,
    qt, gt, qs, gs, qt2, gt2, qs2, gs2, dqt, dst, pt, l2, delta,
    rx1r, rx1b, s1r, s1b, tx2r, tx2b, rx2r, rx2b, tx3r, tx3b, rx3r, rx3b, rx4,
    loc, zs, zr, ys, yr, cs, cr, a_s, a_r, b_s, b_r, c_s, c_r, d_s, d_r,
):
    at = Place(cols)
    O, I, C = at.O, at.I, at.C
    rb = root.shape[0]
    nb, bb, _ = branch.shape
    blen = branch_all.shape[1]
    tok = q.shape[0]
    scale = HD ** (-0.5)
    kinds = (0, 1)
    rx1, s1 = (rx1r, rx1b), (s1r, s1b)
    tx2, rx2, tx3, rx3 = (tx2r, tx2b), (rx2r, rx2b), (tx3r, tx3b), (rx3r, rx3b)
    out = (root_out, branch_out)

    def part(pair, k, i):
        if k == 0:
            return pair[0].at[pl.ds(pl.multiple_of(i * rb, rb), rb)]
        return pair[1].at[:, pl.ds(pl.multiple_of(i * bb, bb), bb)]

    everything = (root_all, branch_all)
    grads = (root_g, branch_g)
    own = (root, branch)
    me = at.index(0, 0, 0)

    def copy(src, dst, ss, rs, dev):
        return pltpu.make_async_remote_copy(
            src_ref=src, dst_ref=dst, send_sem=ss, recv_sem=rs, device_id=dev, device_id_type=MESH
        )

    def z_copy(k, dz, i):
        src = part(everything, k, i)
        return copy(src, src, zs.at[dz, k], zr.at[dz, k], at.dev(dz, 0, 0))

    def y_copy(k, dy, dz, i):
        src = part(everything, k, i)
        slot = dy * O + dz
        return copy(src, src, ys.at[slot, k], yr.at[slot, k], at.dev(0, dy, 0))

    def c_copy(k, slot, i):
        src = part(everything, k, i)
        return copy(src, src, cs.at[slot, k], cr.at[slot, k], at.dev(0, 0, 1))

    def own_copies(k):
        dst = part(everything, k, me)
        made = [copy(own[k], dst, zs.at[d, k], zr.at[d, k], at.dev(d, 0, 0)) for d in range(1, O)]
        made += [
            copy(own[k], dst, ys.at[d * O, k], yr.at[d * O, k], at.dev(0, d, 0)) for d in range(1, I)
        ]
        if C > 1:
            made.append(copy(own[k], dst, cs.at[0, k], cr.at[0, k], at.dev(0, 0, 1)))
        return made

    def z_forward(k, dz):
        i = at.index(-dz, 0, 0)
        z_copy(k, dz, i).wait_recv()
        for dy in range(1, I):
            y_copy(k, dy, dz, i).start()
        if C > 1:
            c_copy(k, dz, i).start()

    def y_forward(k, dy, dz):
        i = at.index(-dz, -dy, 0)
        y_copy(k, dy, dz, i).wait_recv()
        if C > 1:
            c_copy(k, dy * O + dz, i).start()

    def c_arrive(k, dy, dz):
        if C > 1:
            c_copy(k, dy * O + dz, at.index(-dz, -dy, 1)).wait_recv()

    locals_ = [
        pltpu.make_async_copy(a, b, loc.at[n])
        for n, (a, b) in enumerate(
            [(q_in, q), (g_in, g), (o_in, o), (leaf_in, leaf)]
            + [(own[k], part(everything, k, me)) for k in kinds]
        )
    ]
    for cp in locals_:
        cp.start()
    at.greet(rows)
    sent = []
    for k in kinds:
        for cp in own_copies(k):
            cp.start()
            sent.append(cp)
    for cp in locals_:
        cp.wait()

    row = at.row
    seg_row = seg[...]
    tb = jnp.zeros(seg_row.shape, jnp.int32)
    for s in range(segb_ref.shape[1]):
        tb = jnp.where(seg_row == s, segb_ref[0, s], tb)
    length = jnp.zeros(seg_row.shape, jnp.int32)
    for b in range(nb):
        length = jnp.where(tb == b, lens_ref[row * nb + b], length)
    tb_f = jnp.broadcast_to(tb.astype(F32), (HD, tok))
    tb_c = tb_f.T
    l2[...] = ln_t[...] * LOG2E
    for h in range(HEADS):
        hd = slice(h * HD, (h + 1) * HD)
        ht = slice(h * tok, (h + 1) * tok)
        qh = q[:, hd]
        gh = g[:, hd]
        qht = qh.T
        ght = gh.T
        delta[h : h + 1, :] = jnp.sum((gh.astype(F32) * o[:, hd].astype(F32)).T, axis=0, keepdims=True)
        qs[ht, :] = qh
        gs[ht, :] = gh
        qt[:, ht] = qht
        gt[:, ht] = ght
        for b in range(nb):
            bd = slice(b * HD, (b + 1) * HD)
            qs2[ht, bd] = jnp.where(tb_c == b, qh.astype(F32), 0.0).astype(BF16)
            gs2[ht, bd] = jnp.where(tb_c == b, gh.astype(F32), 0.0).astype(BF16)
            qt2[bd, ht] = jnp.where(tb_f == b, qht.astype(F32), 0.0).astype(BF16)
            gt2[bd, ht] = jnp.where(tb_f == b, ght.astype(F32), 0.0).astype(BF16)

    def block(k, v, qtr, gtr, qsr, gsr, allowed):
        n = k.shape[0]
        for h in range(HEADS):
            ht = slice(h * tok, (h + 1) * tok)
            w = jnp.exp2(dot(k, qtr[:, ht]) * (scale * LOG2E) - l2[h : h + 1, :])
            if allowed is not None:
                w = jnp.where(allowed, w, 0.0)
            d = w * (dot(v, gtr[:, ht]) - delta[h : h + 1, :])
            pt[:n, ht] = w.astype(BF16)
            dst[:n, ht] = d.astype(BF16)
        ds = dst[:n]
        return dot(ds, qsr[...]) * scale, dot(pt[:n], gsr[...]), dot(k.T, ds)

    for dz in range(1, O):
        z_forward(0, dz)

    iota_k = lax.broadcasted_iota(jnp.int32, (tok, tok), 0)
    iota_t = lax.broadcasted_iota(jnp.int32, (tok, tok), 1)
    seg_b = jnp.broadcast_to(seg_row.astype(F32), (tok, tok))
    dk, dv, dqp = block(
        leaf[:, :HD], leaf[:, HD:], qt, gt, qs, gs, (seg_b == seg_b.T) & (iota_k <= iota_t)
    )
    leaf_g[:, :HD] = dk
    leaf_g[:, HD:] = dv
    dqt[...] = dqp

    for dy in range(1, I):
        for dz in range(O):
            y_forward(0, dy, dz)

    def mate_copy(k, chip):
        return copy(
            part(grads, k, chip * C + lax.rem(at.c + 1, C)), rx1[k].at[chip],
            a_s.at[chip, k], a_r.at[chip, k], at.dev(0, 0, 1),
        )

    rc = rb * C

    @pl.loop(0, O * I)
    def _(s):
        dz = lax.rem(s, O)
        dy = s // O

        @pl.when((dy == 0) & (dz > 0))
        def _():
            z_forward(1, dz)

        @pl.when(dy > 0)
        def _():
            i = at.index(-dz, -dy, 0)
            slot = dy * O + dz
            src = part(everything, 1, i)
            copy(src, src, ys.at[slot, 1], yr.at[slot, 1], at.dev(0, 0, 1)).wait_recv()
            if C > 1:
                c_copy(1, slot, i).start()

        c_arrive(0, dy, dz)
        chip = at.index(-dz, -dy, 0) // C
        keys = pl.ds(pl.multiple_of(chip * rc, rc), rc)
        dk, dv, dqp = block(root_all[keys, :HD], root_all[keys, HD:], qt, gt, qs, gs, None)
        root_g[keys, :HD] = dk
        root_g[keys, HD:] = dv
        dqt[...] += dqp
        if C > 1:
            mate_copy(0, chip).start()

    for dy in range(I):
        for dz in range(O):
            c_arrive(1, dy, dz)

    far = sorted(range(1, O), key=lambda d: -min(d, O - d)) + [0]
    pairs = [(dy, dz) for dy in list(range(1, I)) + [0] for dz in far]

    def second_copy(k, dy, dz):
        n = dy * O + dz - O
        return copy(
            tx2[k].at[n], rx2[k].at[n], b_s.at[n + O, k], b_r.at[n + O, k], at.dev(0, dy, 0)
        )

    def second(k):
        for dy, dz in pairs:
            i = at.index(dz, dy, 0)
            v = part(grads, k, i)[...]
            if C > 1:
                mate_copy(k, i // C).wait_recv()
                v = v + rx1[k][i // C]
            if dy == 0:
                s1[k][dz] = v
            else:
                tx2[k][dy * O + dz - O] = v.astype(BF16)
                second_copy(k, dy, dz).start()

    def third_copy(k, dz):
        return copy(
            tx3[k].at[dz - 1], rx3[k].at[dz - 1], c_s.at[dz, k], c_r.at[dz, k], at.dev(dz, 0, 0)
        )

    def third(k):
        for dz in far:
            total = s1[k][dz]
            for dy in range(1, I):
                second_copy(k, dy, dz).wait_recv()
                total = total + rx2[k][dy * O + dz - O].astype(F32)
            if dz == 0:
                s1[k][0] = total
            else:
                tx3[k][dz - 1] = total.astype(BF16)
                third_copy(k, dz).start()

    def last(k):
        total = s1[k][0]
        for dz in far[::-1][1:]:
            third_copy(k, dz).wait_recv()
            total = total + rx3[k][dz - 1].astype(F32)
        return total

    second(0)

    per = KB // (bb * C)

    @pl.loop(0, blen // KB)
    def _(i):
        keys = pl.ds(pl.multiple_of(i * KB, KB), KB)
        pos = i * KB + lax.broadcasted_iota(jnp.int32, (KB, tok), 0)
        k = jnp.concatenate([branch_all[b, keys, :HD] for b in range(nb)], axis=1)
        v = jnp.concatenate([branch_all[b, keys, HD:] for b in range(nb)], axis=1)
        dk, dv, dqp = block(k, v, qt2, gt2, qs2, gs2, pos < length)
        for b in range(nb):
            bd = slice(b * HD, (b + 1) * HD)
            branch_g[b, keys, :HD] = dk[:, bd]
            branch_g[b, keys, HD:] = dv[:, bd]
        for h in range(HEADS):
            ht = slice(h * tok, (h + 1) * tok)
            piece = dqp[:HD, ht]
            for b in range(1, nb):
                piece = jnp.where(tb_f == b, dqp[b * HD : (b + 1) * HD, ht], piece)
            dqt[:, ht] += piece
        if C > 1:
            for n in range(per):
                mate_copy(1, i * per + n).start()

    third(0)
    second(1)
    for h in range(HEADS):
        dq[:, h * HD : (h + 1) * HD] = (dqt[:, h * tok : (h + 1) * tok].T * scale).astype(BF16)

    rx4[row] = last(0)
    col = lax.axis_index("cols")

    def row_copy(dr, slot):
        dev = (lax.rem(row + dr, rows), col)
        return copy(rx4.at[slot], rx4.at[slot], d_s.at[dr], d_r.at[dr], dev)

    for dr in range(1, rows):
        row_copy(dr, row).start()
    third(1)
    for dr in range(1, rows):
        row_copy(dr, lax.rem(row + rows - dr, rows)).wait_recv()
    total = rx4[0]
    for n in range(1, rows):
        total = total + rx4[n]
    root_out[...] = total
    branch_out[...] = last(1)

    for cp in sent:
        cp.wait_send()
    for k in kinds:
        for dz in range(1, O):
            i = at.index(-dz, 0, 0)
            for dy in range(1, I):
                y_copy(k, dy, dz, i).wait_send()
            third_copy(k, dz).wait_send()
        for dy in range(I):
            for dz in range(O):
                if C > 1:
                    if dy + dz > 0:
                        c_copy(k, dy * O + dz, at.index(-dz, -dy, 0)).wait_send()
                    mate_copy(k, dy * O + dz).wait_send()
                if dy > 0:
                    second_copy(k, dy, dz).wait_send()
    for dr in range(1, rows):
        row_copy(dr, row).wait_send()


def shards(rows, cols, q, o, g, log_norm, leaf, root, branch, lens, seg, segb):
    O, I, C = split_cols(cols)
    slots = O * I
    tok = q.shape[0]
    n = tok * HEADS
    rb, kw = root.shape
    nb, bb, _ = branch.shape
    rest = max(slots - O, 1)
    rim = max(O - 1, 1)
    dma = pltpu.SemaphoreType.DMA
    V = pltpu.VMEM
    any_ = pl.BlockSpec(memory_space=pl.ANY)
    big = max(KB, tok, rb * C)

    def both(lead, dtype):
        return [V((lead, rb, kw), dtype), V((lead, nb, bb, kw), dtype)]

    return pl.pallas_call(
        functools.partial(fused_kernel, rows, cols),
        out_shape=(
            jax.ShapeDtypeStruct(q.shape, BF16),
            jax.ShapeDtypeStruct(leaf.shape, F32),
            jax.ShapeDtypeStruct(root.shape, F32),
            jax.ShapeDtypeStruct(branch.shape, F32),
        ),
        in_specs=[SMEM] * 2 + [any_] * 3 + [VMEM] + [any_] * 3 + [VMEM],
        out_specs=(VMEM,) * 4,
        scratch_shapes=[
            V(q.shape, BF16), V(q.shape, BF16), V(q.shape, BF16), V(leaf.shape, BF16),
            V((rb * cols, kw), BF16), V((nb, bb * cols, kw), BF16),
            V((rb * cols, kw), F32), V((nb, bb * cols, kw), F32),
            V((HD, n), BF16), V((HD, n), BF16), V((n, HD), BF16), V((n, HD), BF16),
            V((nb * HD, n), BF16), V((nb * HD, n), BF16),
            V((n, nb * HD), BF16), V((n, nb * HD), BF16),
            V((HD, n), F32), V((big, n), BF16), V((big, n), BF16),
            V((HEADS, tok), F32), V((HEADS, tok), F32),
            *both(slots, F32), *both(O, F32), *both(rest, BF16), *both(rest, BF16),
            *both(rim, BF16), *both(rim, BF16), V((rows, rb, kw), F32),
            dma((6,)), dma((O, 2)), dma((O, 2)),
            *[dma((slots, 2)) for _ in range(8)],
            dma((O, 2)), dma((O, 2)), dma((rows,)), dma((rows,)),
        ],
        compiler_params=pltpu.CompilerParams(
            collective_id=0, has_side_effects=True, vmem_limit_bytes=56 << 20
        ),
        name="fused_grads",
    )(lens, segb, q, o, g, log_norm.T, leaf, root, branch, seg)


def solution(mesh):
    both = P(("rows", "cols"), None)
    in_specs = (
        both, both, both, both, both, P("cols", None), P("rows", "cols", None), P(), both, both,
    )
    out_specs = (both, both, P("cols", None), P("rows", "cols", None))
    body = functools.partial(shards, mesh.shape["rows"], mesh.shape["cols"])
    return jax.shard_map(body, mesh=mesh, in_specs=in_specs, out_specs=out_specs, check_vma=False)
```

time: 290 us -> 60.4 us (0.21)
  waiting for transfers between devices: 164 us -> 0 us
  matrix products: 66.6 us -> 0 us
  Pallas kernels: 0 us -> 55 us
  local copies, waits for them, and re-layouts: 32.1 us -> 4.52 us
  between operations: 13.9 us -> 0.65 us
  other arithmetic: 6.25 us -> 0 us
  loops' own time: 5.64 us -> 0 us
    reduce_scatter x2 -> x0, waiting for transfers between devices: 92.4 us -> none  [the longest x1 60.3 us: shards(): lax.psum_scatter(branch_grads, 'cols', scatter_dimension=1, tiled=True)]
    dot_general x45 -> x0, matrix products: 66.6 us -> none  [the longest x9 22.4 us: block_grads(): jnp.einsum('thk,kd->thd', dscore_b, keys_part, preferred_element_type=jnp...]
    pallas_call x0 -> x1, Pallas kernels: none -> 55 us  [shards(): pl.pallas_call(functools.partial(fused_kernel, rows, cols), out_shape=(ja...]
    all_gather x2 -> x0, waiting for transfers between devices: 47.5 us -> none  [the longest x1 36.6 us: shards(): piece = lax.all_gather(branch_kv, 'cols', axis=1, tiled=True)]
    psum x1 -> x0, waiting for transfers between devices: 22.6 us -> none  [shards(): row_whole = lax.psum(root_grads, 'rows')]
    dynamic_update_slice x16 -> x0, local copies, waits for them, and re-layouts: 8.34 us -> none  [sweep_keys(): lax.scan(visit_block, start_sum, jnp.arange(count_rows // block_rows, dty...]
    another operation x3 -> x0, loops' own time: 5.64 us -> none  [sweep_keys(): lax.scan(visit_block, start_sum, jnp.arange(count_rows // block_rows, dty...]
    dynamic_slice x9 -> x0, local copies, waits for them, and re-layouts: 5.5 us -> none  [the longest x8 4.77 us: sweep_keys(): lax.scan(visit_block, start_sum, jnp.arange(count_rows // block_rows, dty...]
  transfers between devices with their start and end apart: 5 -> 0, of which waited for: 5 -> 0; matrix products, arithmetic and copies ran while one was open for 22% -> 0% of each run, Pallas kernels for 0% -> 0%
where the time goes in v2:
time: 60.4 us; the launch traced here: 60.1 us
  Pallas kernels  55 us (91%)
  local copies, waits for them, and re-layouts  4.52 us (7%)
  between operations  0.65 us (1%)
    pallas_call x1, Pallas kernels, shards(): pl.pallas_call(functools.partial(fused_kernel, rows, cols), out_shape=(ja...  55 us
    unnamed x10, local copies, waits for them, and re-layouts  4.52 us

profile of v2, /device:TPU:0, one launch (start us, length us, event | category | flops | bytes accessed | tf_op | source)
XLA Modules:
  0.0 60.1 jit_solution(15513367505955201872)
XLA Ops:
  0.6 55.0 %fused_grads.1 = (bf16[256,1024]{1,0:T(8,128)(2,1)}, f32[256,256]{1,0:T(8,128)}, f32[128,256]{1,0:T(8,128)}, f32[2,64,256]{2,1,0:T(8,128)}) custom-call(s32[4]{0:T(128)} %lens_ref.1, s32[1,8]{1,0:T(1,128)} %segb_ref.1, bf16[256,1024]{1,0:T(8,128)(2,1)} %q_in.1, bf16[256,1024]{1,0:T(8,128)(2,1)} %o_in.1, bf16[256,1024]{1,0:T(8,128)(2,1)} %g_in.1, ...), custom_call_target="tpu_custom_call" | custom-call | tf_op jit(solution)/shard_map/fused_grads/pallas_call | solution.py:389
  55.6 0.0 copy-start
  55.6 1.9 %copy.18 = bf16[256,1024]{1,0:T(8,128)(2,1)} copy(bf16[256,1024]{1,0:T(8,128)(2,1)} %get-tuple-element.8) | data formatting | bytes 1048576
  57.5 0.0 copy-done
  57.5 0.0 copy-start.2
  57.5 0.7 %copy.19 = f32[256,256]{1,0:T(8,128)} copy(f32[256,256]{1,0:T(8,128)S(1)} %copy-done) | data formatting | bytes 524288
  58.2 0.3 copy-done.2
  58.5 0.0 copy-start.1
  58.5 0.7 %copy.20 = f32[128,256]{1,0:T(8,128)} copy(f32[128,256]{1,0:T(8,128)S(1)} %copy-done.2) | data formatting | bytes 262144
  59.2 0.3 copy-done.1
  59.5 0.7 %copy.21 = f32[2,64,256]{2,1,0:T(8,128)} copy(f32[2,64,256]{2,1,0:T(8,128)S(1)} %copy-done.1) | data formatting | bytes 262144
Async XLA Ops:
  55.6 1.9 %copy-start = (f32[256,256]{1,0:T(8,128)S(1)}, f32[256,256]{1,0:T(8,128)}, u32[]{:S(2)}) copy-start(f32[256,256]{1,0:T(8,128)} %get-tuple-element.9) | copy-start | bytes 786436
  57.5 1.0 %copy-start.2 = (f32[128,256]{1,0:T(8,128)S(1)}, f32[128,256]{1,0:T(8,128)}, u32[]{:S(2)}) copy-start(f32[128,256]{1,0:T(8,128)} %get-tuple-element.10) | copy-start | bytes 393220
  58.5 1.0 %copy-start.1 = (f32[2,64,256]{2,1,0:T(8,128)S(1)}, f32[2,64,256]{2,1,0:T(8,128)}, u32[]{:S(2)}) copy-start(f32[2,64,256]{2,1,0:T(8,128)} %get-tuple-element.11) | copy-start | bytes 393220

commit v3 on v2

--- a/solution.py
+++ b/solution.py
@@ -148,10 +148,9 @@
         cp.start()
     at.greet(rows)
     sent = []
-    for k in kinds:
-        for cp in own_copies(k):
-            cp.start()
-            sent.append(cp)
+    for cp in own_copies(0):
+        cp.start()
+        sent.append(cp)
     for cp in locals_:
         cp.wait()
 
@@ -200,6 +199,9 @@
 
     for dz in range(1, O):
         z_forward(0, dz)
+    for cp in own_copies(1):
+        cp.start()
+        sent.append(cp)
 
     iota_k = lax.broadcasted_iota(jnp.int32, (tok, tok), 0)
     iota_t = lax.broadcasted_iota(jnp.int32, (tok, tok), 1)
@@ -211,10 +213,6 @@
     leaf_g[:, HD:] = dv
     dqt[...] = dqp
 
-    for dy in range(1, I):
-        for dz in range(O):
-            y_forward(0, dy, dz)
-
     def mate_copy(k, chip):
         return copy(
             part(grads, k, chip * C + lax.rem(at.c + 1, C)), rx1[k].at[chip],
@@ -223,23 +221,51 @@
 
     rc = rb * C
 
+    def second_copy(k, dy, dz):
+        n = dy * O + dz - O
+        return copy(
+            tx2[k].at[n], rx2[k].at[n], b_s.at[n + O, k], b_r.at[n + O, k], at.dev(0, dy, 0)
+        )
+
+    def second(k, chip):
+        dz = lax.rem(chip // I - at.z + O, O)
+        dy = lax.rem(lax.rem(chip, I) - at.y + I, I)
+        v = part(grads, k, chip * C + at.c)[...]
+        if C > 1:
+            mate_copy(k, chip).wait_recv()
+            v = v + rx1[k][chip]
+
+        @pl.when(dy == 0)
+        def _():
+            s1[k][dz] = v
+
+        if I > 1:
+
+            @pl.when(dy > 0)
+            def _():
+                tx2[k][dy * O + dz - O] = v.astype(BF16)
+                second_copy(k, dy, dz).start()
+
     @pl.loop(0, O * I)
     def _(s):
         dz = lax.rem(s, O)
         dy = s // O
 
+        if I > 1:
+
+            @pl.when(dy < I - 1)
+            def _():
+                y_forward(0, dy + 1, dz)
+
         @pl.when((dy == 0) & (dz > 0))
         def _():
             z_forward(1, dz)
 
-        @pl.when(dy > 0)
-        def _():
-            i = at.index(-dz, -dy, 0)
-            slot = dy * O + dz
-            src = part(everything, 1, i)
-            copy(src, src, ys.at[slot, 1], yr.at[slot, 1], at.dev(0, 0, 1)).wait_recv()
-            if C > 1:
-                c_copy(1, slot, i).start()
+        if I > 1:
+
+            @pl.when(dy > 0)
+            def _():
+                y_forward(1, dy, dz)
 
         c_arrive(0, dy, dz)
         chip = at.index(-dz, -dy, 0) // C
@@ -251,31 +277,16 @@
         if C > 1:
             mate_copy(0, chip).start()
 
+        @pl.when(s > 0)
+        def _():
+            p = s - 1
+            second(0, at.index(-lax.rem(p, O), -(p // O), 0) // C)
+
     for dy in range(I):
         for dz in range(O):
             c_arrive(1, dy, dz)
 
     far = sorted(range(1, O), key=lambda d: -min(d, O - d)) + [0]
-    pairs = [(dy, dz) for dy in list(range(1, I)) + [0] for dz in far]
-
-    def second_copy(k, dy, dz):
-        n = dy * O + dz - O
-        return copy(
-            tx2[k].at[n], rx2[k].at[n], b_s.at[n + O, k], b_r.at[n + O, k], at.dev(0, dy, 0)
-        )
-
-    def second(k):
-        for dy, dz in pairs:
-            i = at.index(dz, dy, 0)
-            v = part(grads, k, i)[...]
-            if C > 1:
-                mate_copy(k, i // C).wait_recv()
-                v = v + rx1[k][i // C]
-            if dy == 0:
-                s1[k][dz] = v
-            else:
-                tx2[k][dy * O + dz - O] = v.astype(BF16)
-                second_copy(k, dy, dz).start()
 
     def third_copy(k, dz):
         return copy(
@@ -301,11 +312,12 @@
             total = total + rx3[k][dz - 1].astype(F32)
         return total
 
-    second(0)
+    second(0, at.index(-(O - 1), -(I - 1), 0) // C)
 
     per = KB // (bb * C)
-
-    @pl.loop(0, blen // KB)
+    steps = blen // KB
+
+    @pl.loop(0, steps)
     def _(i):
         keys = pl.ds(pl.multiple_of(i * KB, KB), KB)
         pos = i * KB + lax.broadcasted_iota(jnp.int32, (KB, tok), 0)
@@ -326,8 +338,18 @@
             for n in range(per):
                 mate_copy(1, i * per + n).start()
 
-    third(0)
-    second(1)
+        @pl.when(i > 0)
+        def _():
+            for n in range(per):
+                second(1, (i - 1) * per + n)
+
+        @pl.when(i == min(2, steps - 1))
+        def _():
+            third(0)
+
+    for n in range(per):
+        second(1, (steps - 1) * per + n)
+    third(1)
     for h in range(HEADS):
         dq[:, h * HD : (h + 1) * HD] = (dqt[:, h * tok : (h + 1) * tok].T * scale).astype(BF16)
 
@@ -340,7 +362,6 @@
 
     for dr in range(1, rows):
         row_copy(dr, row).start()
-    third(1)
     for dr in range(1, rows):
         row_copy(dr, lax.rem(row + rows - dr, rows)).wait_recv()
     total = rx4[0]

time: 60.4 us -> 56.9 us (0.942)
  the two profiles are of different devices: /device:TPU:0 before, /device:TPU:12 now
where the time goes in v3:
time: 56.9 us; the launch traced here: 56.7 us
  Pallas kernels  51.5 us (91%)
  local copies, waits for them, and re-layouts  4.52 us (8%)
  between operations  0.65 us (1%)
    pallas_call x1, Pallas kernels, shards(): pl.pallas_call(functools.partial(fused_kernel, rows, cols), out_shape=(ja...  51.5 us
    unnamed x10, local copies, waits for them, and re-layouts  4.52 us

profile of v3, /device:TPU:12, one launch (start us, length us, event | category | flops | bytes accessed | tf_op | source)
XLA Modules:
  0.0 56.7 jit_solution(18001175511860256668)
XLA Ops:
  0.6 51.5 %fused_grads.1 = (bf16[256,1024]{1,0:T(8,128)(2,1)}, f32[256,256]{1,0:T(8,128)}, f32[128,256]{1,0:T(8,128)}, f32[2,64,256]{2,1,0:T(8,128)}) custom-call(s32[4]{0:T(128)} %lens_ref.1, s32[1,8]{1,0:T(1,128)} %segb_ref.1, bf16[256,1024]{1,0:T(8,128)(2,1)} %q_in.1, bf16[256,1024]{1,0:T(8,128)(2,1)} %o_in.1, bf16[256,1024]{1,0:T(8,128)(2,1)} %g_in.1, ...), custom_call_target="tpu_custom_call" | custom-call | tf_op jit(solution)/shard_map/fused_grads/pallas_call | solution.py:410
  52.1 0.0 copy-start
  52.1 1.9 %copy.18 = bf16[256,1024]{1,0:T(8,128)(2,1)} copy(bf16[256,1024]{1,0:T(8,128)(2,1)} %get-tuple-element.8) | data formatting | bytes 1048576
  54.1 0.0 copy-done
  54.1 0.0 copy-start.2
  54.1 0.7 %copy.19 = f32[256,256]{1,0:T(8,128)} copy(f32[256,256]{1,0:T(8,128)S(1)} %copy-done) | data formatting | bytes 524288
  54.8 0.3 copy-done.2
  55.1 0.0 copy-start.1
  55.1 0.7 %copy.20 = f32[128,256]{1,0:T(8,128)} copy(f32[128,256]{1,0:T(8,128)S(1)} %copy-done.2) | data formatting | bytes 262144
  55.7 0.3 copy-done.1
  56.0 0.7 %copy.21 = f32[2,64,256]{2,1,0:T(8,128)} copy(f32[2,64,256]{2,1,0:T(8,128)S(1)} %copy-done.1) | data formatting | bytes 262144
Async XLA Ops:
  52.1 1.9 %copy-start = (f32[256,256]{1,0:T(8,128)S(1)}, f32[256,256]{1,0:T(8,128)}, u32[]{:S(2)}) copy-start(f32[256,256]{1,0:T(8,128)} %get-tuple-element.9) | copy-start | bytes 786436
  54.1 1.0 %copy-start.2 = (f32[128,256]{1,0:T(8,128)S(1)}, f32[128,256]{1,0:T(8,128)}, u32[]{:S(2)}) copy-start(f32[128,256]{1,0:T(8,128)} %get-tuple-element.10) | copy-start | bytes 393220
  55.1 1.0 %copy-start.1 = (f32[2,64,256]{2,1,0:T(8,128)S(1)}, f32[2,64,256]{2,1,0:T(8,128)}, u32[]{:S(2)}) copy-start(f32[2,64,256]{2,1,0:T(8,128)} %get-tuple-element.11) | copy-start | bytes 393220

commit v4 on v3

--- a/solution.py
+++ b/solution.py
@@ -257,10 +257,6 @@
             def _():
                 y_forward(0, dy + 1, dz)
 
-        @pl.when((dy == 0) & (dz > 0))
-        def _():
-            z_forward(1, dz)
-
         if I > 1:
 
             @pl.when(dy > 0)
@@ -276,6 +272,10 @@
         dqt[...] += dqp
         if C > 1:
             mate_copy(0, chip).start()
+
+        @pl.when((dy == 0) & (dz > 0))
+        def _():
+            z_forward(1, dz)
 
         @pl.when(s > 0)
         def _():

time: 56.9 us -> 55.4 us (0.974)
  Pallas kernels: 51.5 us -> 50 us
    pallas_call x1, Pallas kernels: 51.5 us -> 50 us  [shards(): pl.pallas_call(functools.partial(fused_kernel, rows, cols), out_shape=(ja...]
where the time goes in v4:
time: 55.4 us; the launch traced here: 55.2 us
  Pallas kernels  50 us (90%)
  local copies, waits for them, and re-layouts  4.52 us (8%)
  between operations  0.65 us (1%)
    pallas_call x1, Pallas kernels, shards(): pl.pallas_call(functools.partial(fused_kernel, rows, cols), out_shape=(ja...  50 us
    unnamed x10, local copies, waits for them, and re-layouts  4.52 us

profile of v4, /device:TPU:12, one launch (start us, length us, event | category | flops | bytes accessed | tf_op | source)
XLA Modules:
  0.0 55.2 jit_solution(3999961074951509023)
XLA Ops:
  0.6 50.0 %fused_grads.1 = (bf16[256,1024]{1,0:T(8,128)(2,1)}, f32[256,256]{1,0:T(8,128)}, f32[128,256]{1,0:T(8,128)}, f32[2,64,256]{2,1,0:T(8,128)}) custom-call(s32[4]{0:T(128)} %lens_ref.1, s32[1,8]{1,0:T(1,128)} %segb_ref.1, bf16[256,1024]{1,0:T(8,128)(2,1)} %q_in.1, bf16[256,1024]{1,0:T(8,128)(2,1)} %o_in.1, bf16[256,1024]{1,0:T(8,128)(2,1)} %g_in.1, ...), custom_call_target="tpu_custom_call" | custom-call | tf_op jit(solution)/shard_map/fused_grads/pallas_call | solution.py:410
  50.7 0.0 copy-start
  50.7 1.9 %copy.18 = bf16[256,1024]{1,0:T(8,128)(2,1)} copy(bf16[256,1024]{1,0:T(8,128)(2,1)} %get-tuple-element.8) | data formatting | bytes 1048576
  52.6 0.0 copy-done
  52.6 0.0 copy-start.2
  52.6 0.7 %copy.19 = f32[256,256]{1,0:T(8,128)} copy(f32[256,256]{1,0:T(8,128)S(1)} %copy-done) | data formatting | bytes 524288
  53.3 0.3 copy-done.2
  53.6 0.0 copy-start.1
  53.6 0.7 %copy.20 = f32[128,256]{1,0:T(8,128)} copy(f32[128,256]{1,0:T(8,128)S(1)} %copy-done.2) | data formatting | bytes 262144
  54.2 0.3 copy-done.1
  54.5 0.7 %copy.21 = f32[2,64,256]{2,1,0:T(8,128)} copy(f32[2,64,256]{2,1,0:T(8,128)S(1)} %copy-done.1) | data formatting | bytes 262144
Async XLA Ops:
  50.7 1.9 %copy-start = (f32[256,256]{1,0:T(8,128)S(1)}, f32[256,256]{1,0:T(8,128)}, u32[]{:S(2)}) copy-start(f32[256,256]{1,0:T(8,128)} %get-tuple-element.9) | copy-start | bytes 786436
  52.6 1.0 %copy-start.2 = (f32[128,256]{1,0:T(8,128)S(1)}, f32[128,256]{1,0:T(8,128)}, u32[]{:S(2)}) copy-start(f32[128,256]{1,0:T(8,128)} %get-tuple-element.10) | copy-start | bytes 393220
  53.6 1.0 %copy-start.1 = (f32[2,64,256]{2,1,0:T(8,128)S(1)}, f32[2,64,256]{2,1,0:T(8,128)}, u32[]{:S(2)}) copy-start(f32[2,64,256]{2,1,0:T(8,128)} %get-tuple-element.11) | copy-start | bytes 393220
